TPU v7x, 32 devices: a whole 2x2x4 slice. The times are simulated.
32 devices in a mesh: grp: 2 (over y), seq: 4 (over z), zero: 4 (over x, core).
Axes of the slice: x: 2, y: 2, z: 4, core: 2. Of those that a mesh axis runs over, the one named last changes fastest.
Arguments:
- hidden: bfloat16 [8, 512, 1280], P(('grp', 'zero'), 'seq'), parts along dimension 0, may hold values from -6 to 6
- grad_out: bfloat16 [8, 512, 1280], P(('grp', 'zero'), 'seq'), parts along dimension 0, may hold values from -6 to 6
- w_proj: bfloat16 [1280, 148], P('zero'), may hold values from -0.15625 to 0.15625
- conv_w: bfloat16 [4, 1408], P(None, 'zero'), may hold values from -3 to 3
- a_log: float32 [20], replicated, may hold values from -8 to 1, as said below
- dt_bias: float32 [20], replicated, may hold values from -4.5 to -3
Outputs:
- output: bfloat16 [8, 512, 1280], P(('grp', 'zero'), 'seq'), parts along dimension 0
- grad_hidden: bfloat16 [8, 512, 1280], P(('grp', 'zero'), 'seq'), parts along dimension 0
- grad_proj: float32 [2560, 148], P(('grp', 'zero')), parts along dimension 0
- grad_conv: float32 [8, 1408], P('grp', 'zero'), parts along dimension 0
- grad_heads: float32 [4, 20], P('grp'), parts along dimension 0
There are 2 independent parts, one for each index of `grp`. A program takes and returns all parts, laid end to end along the dimension named above; an argument that names none is the same for every part. Nothing has to cross between parts.
Inputs may be any that keep to these rules, and one draw needn't show every extreme that they name: `a_log`: the logarithms of the heads' decay rates.
All inputs are finite; a program needn't handle non-finite values.
Results may differ from a plain program's by a relative error of at most 0.017.
Values may be sent and summed in bfloat16 or wider, within the bound.
A program may use at most 192 MiB of HBM per device.

v0:
```python
import jax
import jax.numpy as jnp
from jax import lax
from jax.sharding import PartitionSpec as P

WIDTH = 1280
STATE = 64
HEAD_DIM = 64
SPAN = 128
KERNEL = 4


def prefix(x, axis, join, neutral, backward):
    count = lax.axis_size(axis)
    place = lax.axis_index(axis)
    ahead = count - 1 - place if backward else place
    gathered = jax.tree.map(
        lambda a, kind: lax.all_gather(a.astype(kind), axis),
        x,
        jax.tree.map(lambda a: jnp.bfloat16 if a.dtype == jnp.float32 else a.dtype, x),
    )
    state = jax.tree.map(lambda a, e: jnp.zeros_like(a) + jnp.asarray(e, a.dtype), x, neutral)

    def one(hop, state):
        source = count - 1 - hop if backward else hop
        return join(
            state,
            jax.tree.map(
                lambda a, own: lax.dynamic_index_in_dim(a, source, 0, False).astype(own.dtype),
                gathered,
                x,
            ),
        )

    return lax.fori_loop(0, ahead, one, state)


def extended(x, sides, width):
    for axis, dim in sides:
        size, length = (lax.axis_size(axis), x.shape[dim])
        up = [(i, (i + 1) % size) for i in range(size - 1)]
        down = [(j, i) for i, j in up]
        last = lax.slice_in_dim(x, length - width, length, axis=dim)
        leading = lax.slice_in_dim(x, 0, width, axis=dim)
        before = lax.ppermute(last, axis, up)
        after = lax.ppermute(leading, axis, down)
        x = jnp.concatenate([before, x, after], axis=dim)
    return x


def combine_states(earlier, later):
    return (earlier[0] * later[0], later[0][..., None, None] * earlier[1] + later[1])


def pass_upward(pieces):
    identity = (jnp.ones_like(pieces[0]), jnp.zeros_like(pieces[1]))
    return prefix(pieces, "seq", combine_states, identity, False)[1]


def pass_downward(pieces):
    identity = (jnp.ones_like(pieces[0]), jnp.zeros_like(pieces[1]))
    return prefix(pieces, "seq", combine_states, identity, True)[1]


def conv_core(ahead_in, dt_raw, filters, a_log, dt_bias):
    length = dt_raw.shape[0]
    head_count = dt_raw.shape[1]
    blocks = length // SPAN
    mixed_sum = filters[0] * ahead_in[KERNEL - 1 : KERNEL - 1 + length]
    for step_back in range(1, KERNEL):
        mixed_sum = (
            mixed_sum
            + filters[step_back]
            * ahead_in[KERNEL - 1 - step_back : KERNEL - 1 - step_back + length]
        )
    active = jax.nn.silu(mixed_sum)
    values = active[:, :WIDTH].astype(jnp.bfloat16).reshape(blocks, SPAN, head_count, HEAD_DIM)
    b_mat = active[:, WIDTH : WIDTH + STATE].astype(jnp.bfloat16).reshape(blocks, SPAN, STATE)
    c_mat = active[:, WIDTH + STATE :].astype(jnp.bfloat16)
    c_blocks = c_mat.reshape(blocks, SPAN, STATE)
    steps_dt = jax.nn.softplus(dt_raw + dt_bias)
    log_decay = -jnp.exp(a_log) * steps_dt
    within = jnp.cumsum(log_decay.reshape(blocks, SPAN, head_count), axis=1).transpose(0, 2, 1)
    dt_blocks = steps_dt.reshape(blocks, SPAN, head_count).transpose(0, 2, 1)
    scores = jnp.einsum("kin,kjn->kij", c_blocks, b_mat, preferred_element_type=jnp.float32)
    causal = jnp.arange(SPAN)[:, None] >= jnp.arange(SPAN)[None, :]
    gap_log = within[:, :, :, None] - within[:, :, None, :]
    decays = jnp.exp(jnp.where(causal, gap_log, -jnp.inf))
    weights = (scores[:, None] * decays * dt_blocks[:, :, None, :]).astype(jnp.bfloat16)
    y_intra = jnp.einsum("khij,kjhp->kihp", weights, values, preferred_element_type=jnp.float32)
    to_end = jnp.exp(within[:, :, -1:] - within) * dt_blocks
    b_weighted = (to_end[..., None] * b_mat[:, None, :, :].astype(jnp.float32)).astype(jnp.bfloat16)
    states = jnp.einsum("khjn,kjhp->khnp", b_weighted, values, preferred_element_type=jnp.float32)
    totals = within[:, :, -1]

    def advance(carried, current):
        return (jnp.exp(current[0])[:, None, None] * carried + current[1], carried)

    last_state, entering = lax.scan(
        advance, jnp.zeros(states.shape[1:], jnp.float32), (totals, states)
    )
    y_inter = jnp.einsum(
        "kin,khnp->kihp", c_blocks.astype(jnp.float32), entering, precision=lax.Precision.HIGH
    )
    y_inter = y_inter * jnp.exp(within).transpose(0, 2, 1)[..., None]
    y_local = (y_intra + y_inter).reshape(length, WIDTH)
    offsets = jnp.cumsum(totals, axis=0) - totals
    reached = jnp.exp(within + offsets[:, :, None]).transpose(0, 2, 1).reshape(length, head_count)
    overall = jnp.exp(jnp.sum(totals, axis=0))
    return (y_local, overall, last_state, reached, c_mat)


def add_incoming(y_local, reached, c_mat, incoming):
    carried = jnp.einsum(
        "tn,hnp->thp", c_mat.astype(jnp.float32), incoming, precision=lax.Precision.HIGH
    )
    return y_local + (reached[:, :, None] * carried).reshape(y_local.shape)


def strand_pass(tokens, cotangent, w_full, filters, a_log, dt_bias):
    length = tokens.shape[1]
    margin = KERNEL - 1
    projected = jnp.einsum("std,dc->stc", tokens, w_full, preferred_element_type=jnp.float32)
    inner_act = jnp.concatenate([tokens, projected[..., : 2 * STATE].astype(jnp.bfloat16)], axis=2)
    dt_raw = projected[..., 2 * STATE :]
    padded = extended(inner_act, (("seq", 1),), margin)
    padded = padded.astype(jnp.float32)
    ahead_in = padded[:, : length + margin]
    behind = jnp.flip(padded[:, margin:], axis=1)
    core_batch = jax.vmap(conv_core, in_axes=(0, 0, None, None, None))
    finish_batch = jax.vmap(add_incoming)
    ahead_out, ahead_back = jax.vjp(core_batch, ahead_in, dt_raw, filters, a_log, dt_bias)
    behind_out, behind_back = jax.vjp(
        core_batch, behind, jnp.flip(dt_raw, axis=1), filters, a_log, dt_bias
    )
    ahead_state = pass_upward((ahead_out[1], ahead_out[2]))
    behind_state = pass_downward((behind_out[1], behind_out[2]))
    y_ahead, ahead_finish = jax.vjp(
        finish_batch, ahead_out[0], ahead_out[3], ahead_out[4], ahead_state
    )
    y_behind, behind_finish = jax.vjp(
        finish_batch, behind_out[0], behind_out[3], behind_out[4], behind_state
    )
    result = (y_ahead + jnp.flip(y_behind, axis=1)).astype(jnp.bfloat16)
    upstream = cotangent.astype(jnp.float32)
    grad_ahead = ahead_finish(upstream)
    grad_behind = behind_finish(jnp.flip(upstream, axis=1))
    later_ahead = pass_downward((ahead_out[1], grad_ahead[3]))
    later_behind = pass_upward((behind_out[1], grad_behind[3]))
    core_ahead = ahead_back(
        (
            grad_ahead[0],
            jnp.sum(later_ahead * ahead_state, axis=(-2, -1)),
            later_ahead,
            grad_ahead[1],
            grad_ahead[2],
        )
    )
    core_behind = behind_back(
        (
            grad_behind[0],
            jnp.sum(later_behind * behind_state, axis=(-2, -1)),
            later_behind,
            grad_behind[1],
            grad_behind[2],
        )
    )
    grad_padded = jnp.pad(core_ahead[0], ((0, 0), (0, margin), (0, 0))) + jnp.pad(
        jnp.flip(core_behind[0], axis=1), ((0, 0), (margin, 0), (0, 0))
    )
    rims = jnp.concatenate([grad_padded[:, :margin], grad_padded[:, length + margin :]], axis=1)
    rims = extended(rims.astype(jnp.bfloat16), (("seq", 1),), margin).astype(rims.dtype)
    own_rows = grad_padded[:, margin : length + margin]
    own_rows = own_rows.at[:, :margin].add(rims[:, :margin])
    own_rows = own_rows.at[:, length - margin :].add(rims[:, 3 * margin :])
    grad_inner = own_rows.astype(jnp.bfloat16)
    grad_dt = core_ahead[1] + jnp.flip(core_behind[1], axis=1)
    grad_projected = jnp.concatenate(
        [grad_inner[..., WIDTH:], grad_dt.astype(jnp.bfloat16)], axis=2
    )
    grad_weight = jnp.einsum(
        "std,stc->dc", tokens, grad_projected, preferred_element_type=jnp.float32
    )
    back_proj = jnp.einsum(
        "stc,dc->std", grad_projected, w_full, preferred_element_type=jnp.float32
    )
    grad_tokens = (grad_inner[..., :WIDTH].astype(jnp.float32) + back_proj).astype(jnp.bfloat16)
    grad_filters = core_ahead[2] + core_behind[2]
    grad_decay = jnp.stack([core_ahead[3] + core_behind[3], core_ahead[4] + core_behind[4]])
    return (result, grad_tokens, grad_weight, grad_filters, grad_decay)


def per_device(hidden, grad_out, w_proj, conv_w, a_log, dt_bias):
    w_full, conv_full = (
        lax.all_gather(w_proj, "zero", axis=0, tiled=True),
        lax.all_gather(conv_w, "zero", axis=1, tiled=True),
    )
    filters = conv_full.astype(jnp.float32)
    first = strand_pass(hidden, grad_out, w_full, filters, a_log, dt_bias)
    second = strand_pass(
        jnp.flip(hidden, axis=2), jnp.flip(grad_out, axis=2), w_full, filters, a_log, dt_bias
    )
    first_out, first_grad = (first[0], first[1])
    other_out = jnp.flip(second[0], axis=2)
    other_grad = jnp.flip(second[1], axis=2)
    grad_weight = first[2] + second[2]
    grad_filters = first[3] + second[3]
    grad_decay = first[4] + second[4]
    output = (first_out.astype(jnp.float32) + other_out.astype(jnp.float32)).astype(jnp.bfloat16)
    grad_hidden = (first_grad.astype(jnp.float32) + other_grad.astype(jnp.float32)).astype(
        jnp.bfloat16
    )
    part_weight, part_filters = (
        lax.psum_scatter(
            grad_weight.astype(jnp.bfloat16), "zero", scatter_dimension=0, tiled=True
        ).astype(jnp.float32),
        lax.psum_scatter(
            grad_filters.astype(jnp.bfloat16), "zero", scatter_dimension=1, tiled=True
        ).astype(jnp.float32),
    )
    share_weight, share_filters = (
        lax.psum(part_weight.astype(jnp.bfloat16), "seq").astype(jnp.float32),
        lax.psum(part_filters.astype(jnp.bfloat16), "seq").astype(jnp.float32),
    )
    grad_heads = lax.psum(grad_decay, ("seq", "zero"))
    return (output, grad_hidden, share_weight, share_filters, grad_heads)


def solution(mesh):
    return jax.shard_map(
        per_device,
        mesh=mesh,
        in_specs=(
            P(("grp", "zero"), "seq", None),
            P(("grp", "zero"), "seq", None),
            P("zero", None),
            P(None, "zero"),
            P(),
            P(),
        ),
        out_specs=(
            P(("grp", "zero"), "seq", None),
            P(("grp", "zero"), "seq", None),
            P(("grp", "zero"), None),
            P("grp", "zero"),
            P("grp", None),
        ),
        check_vma=False,
    )
```

profile of v0, /device:TPU:0, one launch (start us, length us, event | category | flops | bytes accessed | tf_op | source)
XLA Modules:
  0.0 792.8 jit_solution(859587964172044816)
XLA Ops:
  7.2 8.7 %all-gather.13 = bf16[4,320,148]{1,2,0:T(8,128)(2,1)S(1)} all-gather(bf16[1,320,148]{1,2,0:T(8,128)(2,1)} %bitcast.1260), channel_id=1, replica_groups=mesh['grp'=2,'seq'=4,'zero'=4] {'zero'}, dimensions={0}, use_global_device_ids=true | all-gather | bytes 473600 | tf_op jit(solution)/shard_map/all_gather | solution.py:195
  62.5 9.1 %all-gather.6 = bf16[4,1,20,1]{2,3,1,0:T(2,128)(2,1)} all-gather(bf16[1,1,20,1]{2,3,1,0:T(2,128)(2,1)S(1)} %get-tuple-element.1334), channel_id=8, replica_groups=mesh['grp'=2,'seq'=4,'zero'=4] {'seq'}, dimensions={0}, use_global_device_ids=true | all-gather | bytes 200 | tf_op jit(solution)/shard_map/all_gather | solution.py:18
  71.6 8.6 %all-gather.4 = bf16[4,1,20,1]{2,3,1,0:T(2,128)(2,1)} all-gather(bf16[1,1,20,1]{2,3,1,0:T(2,128)(2,1)S(1)} %get-tuple-element.1331), channel_id=6, replica_groups=mesh['grp'=2,'seq'=4,'zero'=4] {'seq'}, dimensions={0}, use_global_device_ids=true | all-gather | bytes 200 | tf_op jit(solution)/shard_map/all_gather | solution.py:18
  80.2 8.9 %all-gather.2 = bf16[4,1,20,1]{2,3,1,0:T(2,128)(2,1)} all-gather(bf16[1,1,20,1]{2,3,1,0:T(2,128)(2,1)S(1)} %get-tuple-element.1328), channel_id=4, replica_groups=mesh['grp'=2,'seq'=4,'zero'=4] {'seq'}, dimensions={0}, use_global_device_ids=true | all-gather | bytes 200 | tf_op jit(solution)/shard_map/all_gather | solution.py:18
  89.2 8.9 %all-gather = bf16[4,1,20,1]{2,3,1,0:T(2,128)(2,1)} all-gather(bf16[1,1,20,1]{2,3,1,0:T(2,128)(2,1)S(1)} %get-tuple-element.1325), channel_id=2, replica_groups=mesh['grp'=2,'seq'=4,'zero'=4] {'seq'}, dimensions={0}, use_global_device_ids=true | all-gather | bytes 200 | tf_op jit(solution)/shard_map/all_gather | solution.py:18
  157.0 6.6 slice.366
  174.2 19.9 %all-gather.7 = bf16[80,64,64]{2,1,0:T(8,128)(2,1)} all-gather(bf16[20,64,64]{2,1,0:T(8,128)(2,1)S(1)} %fusion.28), channel_id=9, replica_groups=mesh['grp'=2,'seq'=4,'zero'=4] {'seq'}, dimensions={0}, use_global_device_ids=true | all-gather | bytes 819200 | tf_op jit(solution)/shard_map/all_gather | solution.py:18
  203.9 19.0 %all-gather.11 = bf16[4,20,64,64]{3,2,1,0:T(8,128)(2,1)} all-gather(bf16[1,20,64,64]{3,2,1,0:T(8,128)(2,1)} %copy.689), channel_id=13, replica_groups=mesh['grp'=2,'seq'=4,'zero'=4] {'seq'}, dimensions={0}, use_global_device_ids=true | all-gather | bytes 819200 | tf_op jit(solution)/shard_map/all_gather | solution.py:18
  239.3 24.0 %all-gather.3 = bf16[80,64,64]{2,1,0:T(8,128)(2,1)} all-gather(bf16[20,64,64]{2,1,0:T(8,128)(2,1)S(1)} %fusion.26), channel_id=5, replica_groups=mesh['grp'=2,'seq'=4,'zero'=4] {'seq'}, dimensions={0}, use_global_device_ids=true | all-gather | bytes 819200 | tf_op jit(solution)/shard_map/all_gather | solution.py:18
  264.2 8.3 %while.69 = (s32[]{:T(128)}, f32[1,20,64,64]{3,2,1,0:T(8,128)}, s32[]{:T(128)}, bf16[4,1,20]{2,1,0:T(2,128)(2,1)}, bf16[4,1,20,64,64]{4,3,2,1,0:T(8,128)(2,1)}, ...) while((s32[]{:T(128)}, f32[1,20,64,64]{3,2,1,0:T(8,128)}, s32[]{:T(128)}, bf16[4,1,20]{2,1,0:T(2,128)(2,1)}, ...), condition=%wide.region_5.7_spmd, body=%wide.region_4.6_spmd.sunk | while | flops 245786 | bytes 819555 | solution.py:35
  276.5 19.0 %all-gather.9 = bf16[4,20,64,64]{3,2,1,0:T(8,128)(2,1)} all-gather(bf16[1,20,64,64]{3,2,1,0:T(8,128)(2,1)} %copy.664), channel_id=11, replica_groups=mesh['grp'=2,'seq'=4,'zero'=4] {'seq'}, dimensions={0}, use_global_device_ids=true | all-gather | bytes 819200 | tf_op jit(solution)/shard_map/all_gather | solution.py:18
  340.2 29.1 %all-gather.10 = bf16[4,20,64,64]{3,2,1,0:T(8,128)(2,1)} all-gather(bf16[1,20,64,64]{3,2,1,0:T(8,128)(2,1)} %copy.684), channel_id=12, replica_groups=mesh['grp'=2,'seq'=4,'zero'=4] {'seq'}, dimensions={0}, use_global_device_ids=true | all-gather | bytes 819200 | tf_op jit(solution)/shard_map/all_gather | solution.py:18
  370.3 8.5 %while.74 = (s32[]{:T(128)}, f32[1,20,64,64]{3,2,1,0:T(8,128)}, s32[]{:T(128)}, bf16[4,1,20]{2,1,0:T(2,128)(2,1)}, bf16[4,1,20,64,64]{4,3,2,1,0:T(8,128)(2,1)}, ...) while((s32[]{:T(128)}, f32[1,20,64,64]{3,2,1,0:T(8,128)}, s32[]{:T(128)}, bf16[4,1,20]{2,1,0:T(2,128)(2,1)}, ...), condition=%wide.region_44.46_spmd, body=%wide.region_43.45_spmd.sunk | while | flops 245786 | bytes 819555 | solution.py:35
  393.5 21.7 %all-gather.8 = bf16[4,20,64,64]{3,2,1,0:T(8,128)(2,1)} all-gather(bf16[1,20,64,64]{3,2,1,0:T(8,128)(2,1)} %copy.659), channel_id=10, replica_groups=mesh['grp'=2,'seq'=4,'zero'=4] {'seq'}, dimensions={0}, use_global_device_ids=true | all-gather | bytes 819200 | tf_op jit(solution)/shard_map/all_gather | solution.py:18
  416.1 8.3 %while.72 = (s32[]{:T(128)}, f32[1,20,64,64]{3,2,1,0:T(8,128)}, s32[]{:T(128)}, bf16[4,1,20]{2,1,0:T(2,128)(2,1)}, bf16[4,1,20,64,64]{4,3,2,1,0:T(8,128)(2,1)}, ...) while((s32[]{:T(128)}, f32[1,20,64,64]{3,2,1,0:T(8,128)}, s32[]{:T(128)}, bf16[4,1,20]{2,1,0:T(2,128)(2,1)}, ...), condition=%wide.region_14.16_spmd, body=%wide.region_13.15_spmd.sunk | while | flops 245786 | bytes 819555 | solution.py:35
  429.0 23.8 %all-gather.5 = bf16[80,64,64]{2,1,0:T(8,128)(2,1)} all-gather(bf16[20,64,64]{2,1,0:T(8,128)(2,1)S(1)} %fusion.27), channel_id=7, replica_groups=mesh['grp'=2,'seq'=4,'zero'=4] {'seq'}, dimensions={0}, use_global_device_ids=true | all-gather | bytes 819200 | tf_op jit(solution)/shard_map/all_gather | solution.py:18
  455.1 26.7 %all-gather.1 = bf16[80,64,64]{2,1,0:T(8,128)(2,1)} all-gather(bf16[20,64,64]{2,1,0:T(8,128)(2,1)S(1)} %fusion.25), channel_id=3, replica_groups=mesh['grp'=2,'seq'=4,'zero'=4] {'seq'}, dimensions={0}, use_global_device_ids=true | all-gather | bytes 819200 | tf_op jit(solution)/shard_map/all_gather | solution.py:18
  507.1 8.0 %reverse.8 = f32[1,256,1408]{1,2,0:T(8,128)} reverse(f32[1,256,1408]{1,2,0:T(8,128)S(1)} %bitcast.1187), dimensions={1} | reverse | bytes 2883584
  525.7 12.4 %reverse.9 = f32[1,256,1408]{1,2,0:T(8,128)} reverse(f32[1,256,1408]{1,2,0:T(8,128)} %bitcast.1188), dimensions={1} | reverse | bytes 2883584
  570.1 6.8 collective-permute-start.6
  697.5 31.7 %psum.23 = f32[2,20]{1,0:T(2,128)} all-reduce(f32[2,20]{1,0:T(2,128)S(1)} %maximum_add_fusion), channel_id=1, replica_groups=mesh['grp'=2,'seq'=4,'zero'=4] {'seq','zero'}, use_global_device_ids=true, to_apply=%region_100.102 | all-reduce | flops 40 | bytes 320 | tf_op jit(solution)/shard_map/psum | solution.py:225
  735.0 12.3 %reduce-scatter.9.cloned.1.call-done = bf16[352,4]{1,0:T(8,128)(2,1)} async-done(((bf16[1408,4]{1,0:T(8,128)(2,1)}), bf16[352,4]{1,0:T(8,128)(2,1)}) %reduce-scatter.9.cloned.1.call-update) | async-done | bytes 2832
  748.3 11.7 %psum.22 = bf16[4,352]{1,0:T(4,128)(2,1)S(1)} all-reduce(bf16[4,352]{1,0:T(4,128)(2,1)S(1)} %copy.719), channel_id=1, replica_groups=mesh['grp'=2,'seq'=4,'zero'=4] {'seq'}, use_global_device_ids=true, to_apply=%region_91.93 | all-reduce | flops 1408 | bytes 5632 | tf_op jit(solution)/shard_map/psum | solution.py:223
  760.6 23.9 %all-reduce.58.cloned.1.call-done = bf16[320,148]{0,1:T(8,128)(2,1)} async-done(((bf16[320,148]{0,1:T(8,128)(2,1)}), bf16[320,148]{0,1:T(8,128)(2,1)}) %all-reduce.58.cloned.1.call-update) | async-done | bytes 94736 | tf_op jit(solution)/shard_map/psum | solution.py:222
  (858 shorter events, 440.1 us)
Async XLA Ops:
  7.2 724.8 %reduce-scatter.7.cloned.1.call-start = ((), (), s32[]{:S(2)}) async-start(), calls=%async_computation.3 | async-start | bytes 819200
  18.1 106.2 %collective-permute-start.1 = (bf16[1,3,1408]{1,2,0:T(8,128)(2,1)}, bf16[1,3,1408]{1,2,0:T(8,128)(2,1)}, u32[]{:S(2)}, u32[]{:S(2)}) collective-permute-start(bf16[1,3,1408]{1,2,0:T(8,128)(2,1)} %get-tuple-element.1305), channel_id=1, source_target_pairs={{4,0},{8,4},{12,8},{5,1},{9,5},{13,9},{6,2},{10,6},{14,10},{7,3},{... | collective-permute-start | bytes 25352 | tf_op jit(solution)/shard_map/ppermute | solution.py:46
  19.4 104.9 %collective-permute-start = (bf16[1,3,1408]{1,2,0:T(8,128)(2,1)}, bf16[1,3,1408]{1,2,0:T(8,128)(2,1)}, u32[]{:S(2)}, u32[]{:S(2)}) collective-permute-start(bf16[1,3,1408]{1,2,0:T(8,128)(2,1)} %get-tuple-element.1304), channel_id=1, source_target_pairs={{0,4},{4,8},{8,12},{1,5},{5,9},{9,13},{2,6},{6,10},{10,14},{3,7},{... | collective-permute-start | bytes 25352 | tf_op jit(solution)/shard_map/ppermute | solution.py:45
  25.1 73.0 %copy-start.25 = (bf16[1,128,1280]{1,2,0:T(8,128)(2,1)}, bf16[1,128,1280]{1,2,0:T(8,128)(2,1)S(1)}, u32[]{:S(2)}) copy-start(bf16[1,128,1280]{1,2,0:T(8,128)(2,1)S(1)} %rev.50) | copy-start | bytes 983044
  26.6 71.6 %collective-permute-start.3 = (bf16[1,3,1408]{1,2,0:T(8,128)(2,1)}, bf16[1,3,1408]{1,2,0:T(8,128)(2,1)}, u32[]{:S(2)}, u32[]{:S(2)}) collective-permute-start(bf16[1,3,1408]{1,2,0:T(8,128)(2,1)} %get-tuple-element.1307), channel_id=1, source_target_pairs={{4,0},{8,4},{12,8},{5,1},{9,5},{13,9},{6,2},{10,6},{14,10},{7,3},{... | collective-permute-start | bytes 25352 | tf_op jit(solution)/shard_map/ppermute | solution.py:46
  27.9 70.3 %collective-permute-start.2 = (bf16[1,3,1408]{1,2,0:T(8,128)(2,1)}, bf16[1,3,1408]{1,2,0:T(8,128)(2,1)}, u32[]{:S(2)}, u32[]{:S(2)}) collective-permute-start(bf16[1,3,1408]{1,2,0:T(8,128)(2,1)} %get-tuple-element.1306), channel_id=1, source_target_pairs={{0,4},{4,8},{8,12},{1,5},{5,9},{9,13},{2,6},{6,10},{10,14},{3,7},{... | collective-permute-start | bytes 25352 | tf_op jit(solution)/shard_map/ppermute | solution.py:45
  33.6 23.5 %copy-start.52 = (f32[1,1,128,20]{3,2,1,0:T(8,128)}, f32[1,1,128,20]{3,2,1,0:T(8,128)S(1)}, u32[]{:S(2)}) copy-start(f32[1,1,128,20]{3,2,1,0:T(8,128)S(1)} %reduce_window_sum.90) | copy-start | bytes 30724
  35.8 24.7 %copy-start.54 = (f32[1,1,128,20]{3,2,1,0:T(8,128)}, f32[1,1,128,20]{3,2,1,0:T(8,128)S(1)}, u32[]{:S(2)}) copy-start(f32[1,1,128,20]{3,2,1,0:T(8,128)S(1)} %reduce_window_sum.86) | copy-start | bytes 30724
  37.2 21.9 %copy-start.56 = (f32[1,1,128,20]{3,2,1,0:T(8,128)}, f32[1,1,128,20]{3,2,1,0:T(8,128)S(1)}, u32[]{:S(2)}) copy-start(f32[1,1,128,20]{3,2,1,0:T(8,128)S(1)} %reduce_window_sum.88) | copy-start | bytes 30724
  38.6 22.6 %copy-start.58 = (f32[1,1,128,20]{3,2,1,0:T(8,128)}, f32[1,1,128,20]{3,2,1,0:T(8,128)S(1)}, u32[]{:S(2)}) copy-start(f32[1,1,128,20]{3,2,1,0:T(8,128)S(1)} %reduce_window_sum.84) | copy-start | bytes 30724
  45.0 80.9 %copy-start.140 = (f32[1408]{0:T(1024)}, f32[1408]{0:T(1024)S(1)}, u32[]{:S(2)}) copy-start(f32[1408]{0:T(1024)S(1)} %get-tuple-element.1150) | copy-start | bytes 16900
  45.1 80.9 %copy-start.142 = (f32[1408]{0:T(1024)}, f32[1408]{0:T(1024)S(1)}, u32[]{:S(2)}) copy-start(f32[1408]{0:T(1024)S(1)} %get-tuple-element.1151) | copy-start | bytes 16900
  199.6 23.3 %copy-start.2 = (f32[1,20,64,64]{3,2,1,0:T(8,128)}, f32[1,20,64,64]{3,2,1,0:T(8,128)S(1)}, u32[]{:S(2)}) copy-start(f32[1,20,64,64]{3,2,1,0:T(8,128)S(1)} %get-tuple-element.760) | copy-start | bytes 983044
  568.8 93.1 %collective-permute-start.7 = (bf16[1,3,1408]{1,2,0:T(8,128)(2,1)}, bf16[1,3,1408]{1,2,0:T(8,128)(2,1)}, u32[]{:S(2)}, u32[]{:S(2)}) collective-permute-start(bf16[1,3,1408]{1,2,0:T(8,128)(2,1)} %get-tuple-element.1271), channel_id=1, source_target_pairs={{4,0},{8,4},{12,8},{5,1},{9,5},{13,9},{6,2},{10,6},{14,10},{7,3},{... | collective-permute-start | bytes 25352 | tf_op jit(solution)/shard_map/ppermute | solution.py:46
  570.1 91.8 %collective-permute-start.6 = (bf16[1,3,1408]{1,2,0:T(8,128)(2,1)}, bf16[1,3,1408]{1,2,0:T(8,128)(2,1)}, u32[]{:S(2)}, u32[]{:S(2)}) collective-permute-start(bf16[1,3,1408]{1,2,0:T(8,128)(2,1)} %get-tuple-element.1270), channel_id=1, source_target_pairs={{0,4},{4,8},{8,12},{1,5},{5,9},{9,13},{2,6},{6,10},{10,14},{3,7},{... | collective-permute-start | bytes 25352 | tf_op jit(solution)/shard_map/ppermute | solution.py:45
  589.2 21.5 %copy-start.123 = (f32[1,1,128,20]{3,2,1,0:T(8,128)}, f32[1,1,128,20]{3,2,1,0:T(8,128)S(1)}, u32[]{:S(2)}) copy-start(f32[1,1,128,20]{3,2,1,0:T(8,128)S(1)} %reduce_window_sum.95) | copy-start | bytes 30724
  591.2 86.8 %collective-permute-start.5 = (bf16[1,3,1408]{1,2,0:T(8,128)(2,1)}, bf16[1,3,1408]{1,2,0:T(8,128)(2,1)}, u32[]{:S(2)}, u32[]{:S(2)}) collective-permute-start(bf16[1,3,1408]{1,2,0:T(8,128)(2,1)} %get-tuple-element.1269), channel_id=1, source_target_pairs={{4,0},{8,4},{12,8},{5,1},{9,5},{13,9},{6,2},{10,6},{14,10},{7,3},{... | collective-permute-start | bytes 25352 | tf_op jit(solution)/shard_map/ppermute | solution.py:46
  592.5 85.5 %collective-permute-start.4 = (bf16[1,3,1408]{1,2,0:T(8,128)(2,1)}, bf16[1,3,1408]{1,2,0:T(8,128)(2,1)}, u32[]{:S(2)}, u32[]{:S(2)}) collective-permute-start(bf16[1,3,1408]{1,2,0:T(8,128)(2,1)} %get-tuple-element.1268), channel_id=1, source_target_pairs={{0,4},{4,8},{8,12},{1,5},{5,9},{9,13},{2,6},{6,10},{10,14},{3,7},{... | collective-permute-start | bytes 25352 | tf_op jit(solution)/shard_map/ppermute | solution.py:45
  639.3 24.9 %copy-start.14 = (f32[1,131,1408]{1,2,0:T(8,128)S(1)}, f32[1,131,1408]{1,2,0:T(8,128)}, u32[]{:S(2)}) copy-start(f32[1,131,1408]{1,2,0:T(8,128)} %copy-done.13) | copy-start | bytes 2213380
  695.0 34.3 %copy-start.88 = (f32[1,128,1280]{2,1,0:T(8,128)S(1)}, f32[1,128,1280]{2,1,0:T(8,128)}, u32[]{:S(2)}) copy-start(f32[1,128,1280]{2,1,0:T(8,128)} %rev.49) | copy-start | bytes 1966084
  695.0 34.3 %copy-start.89 = (f32[1,128,1280]{2,1,0:T(8,128)S(1)}, f32[1,128,1280]{2,1,0:T(8,128)}, u32[]{:S(2)}) copy-start(f32[1,128,1280]{2,1,0:T(8,128)} %copy.618) | copy-start | bytes 1966084
  695.0 34.3 %copy-start.90 = (f32[1,128,1280]{2,1,0:T(8,128)S(1)}, f32[1,128,1280]{2,1,0:T(8,128)}, u32[]{:S(2)}) copy-start(f32[1,128,1280]{2,1,0:T(8,128)} %copy.619) | copy-start | bytes 1966084
  696.1 51.2 %reduce-scatter.9.cloned.1.call-start = ((), (), s32[]{:S(2)}) async-start(), calls=%async_computation.4 | async-start | bytes 450560
  729.2 55.2 %all-reduce.58.cloned.1.call-start = ((), (), s32[]{:S(2)}) async-start(), calls=%async_computation.2 | async-start | bytes 233472 | tf_op jit(solution)/shard_map/psum | solution.py:222
  (246 other events, 1305.6 us)
Sparse Core Ops, SparseCore 0:
  696.3 26.8 reduce-scatter.6
  729.4 17.9 reduce-scatter.8
  750.3 34.0 all-reduce.57
where the time goes:
time: 808 us; the launch traced here: 793 us
  blocking collectives  276 us (34%)
  local copies, waits for them, and re-layouts  219 us (27%)
  other arithmetic  139 us (17%)
  matrix products  75.8 us (9%)
  waiting for transfers between devices  36.3 us (4%)
  starting transfers between devices  28.9 us (4%)
  between operations  17 us (2%)
    all_gather x12, blocking collectives, prefix(): lax.all_gather(a.astype(kind), axis)  219 us
    unnamed x530, local copies, waits for them, and re-layouts  38.1 us
    slice x6, local copies, waits for them, and re-layouts, conv_core(): ahead_in[KERNEL - 1 - step_back:KERNEL - 1 - step_back + length]  37.1 us
    psum x1, blocking collectives, per_device(): grad_heads = lax.psum(grad_decay, ('seq', 'zero'))  31.7 us
    psum x1, waiting for transfers between devices, per_device(): lax.psum(part_weight.astype(jnp.bfloat16), 'seq').astype(jnp.float32)  23.9 us
    ppermute x4, starting transfers between devices, extended(): before = lax.ppermute(last, axis, up)  23.6 us
    add x12, other arithmetic, combine_states(): later[0][..., None, None] * earlier[1] + later[1]  22.9 us
    dot_general x12, matrix products, conv_core(): jnp.einsum('khij,kjhp->kihp', weights, values, preferred_element_type=jnp...  20.9 us
  transfers between devices with their start and end apart: 11, of which 2 were waited for; matrix products, arithmetic and copies ran while one was open for 19% of the time, Pallas kernels for 0%

commit v1 on v0

--- a/solution.py
+++ b/solution.py
@@ -2,12 +2,18 @@
 import jax.numpy as jnp
 from jax import lax
 from jax.sharding import PartitionSpec as P
+from jax.lax import all_gather
 
 WIDTH = 1280
 STATE = 64
 HEAD_DIM = 64
 SPAN = 128
 KERNEL = 4
+
+
+def lift_ticks_all(payload, comm_axis):
+    reply = jnp.sum(all_gather(payload, axis_name=comm_axis), axis=0)
+    return reply
 
 
 def prefix(x, axis, join, neutral, backward):
@@ -219,7 +225,7 @@
         ).astype(jnp.float32),
     )
     share_weight, share_filters = (
-        lax.psum(part_weight.astype(jnp.bfloat16), "seq").astype(jnp.float32),
+        lift_ticks_all(part_weight.astype(jnp.bfloat16), "seq").astype(jnp.float32),
         lax.psum(part_filters.astype(jnp.bfloat16), "seq").astype(jnp.float32),
     )
     grad_heads = lax.psum(grad_decay, ("seq", "zero"))

time: 808 us -> 768 us (0.950)
  waiting for transfers between devices: 36.3 us -> 0.07 us
  local copies, waits for them, and re-layouts: 219 us -> 206 us
  blocking collectives: 276 us -> 286 us
    psum x1 -> x0, waiting for transfers between devices: 23.9 us -> none  [per_device(): lax.psum(part_weight.astype(jnp.bfloat16), 'seq').astype(jnp.float32)]
    all_gather x0 -> x1, blocking collectives: none -> 15.6 us  [lift_ticks_all(): reply = jnp.sum(all_gather(payload, axis_name=comm_axis), axis=0)]
    unnamed x5 -> x4, waiting for transfers between devices: 12.4 us -> 0.04 us
    unnamed x530 -> x490, local copies, waits for them, and re-layouts: 38.1 us -> 37 us
  transfers between devices with their start and end apart: 11 -> 10, of which waited for: 2 -> 0; matrix products, arithmetic and copies ran while one was open for 19% -> 18% of each run, Pallas kernels for 0% -> 0%
where the time goes in v1:
time: 768 us; the launch traced here: 754 us
  blocking collectives  286 us (37%)
  local copies, waits for them, and re-layouts  206 us (27%)
  other arithmetic  139 us (18%)
  matrix products  75 us (10%)
  starting transfers between devices  28.9 us (4%)
  between operations  17.2 us (2%)
    all_gather x12, blocking collectives, prefix(): lax.all_gather(a.astype(kind), axis)  217 us
    slice x6, local copies, waits for them, and re-layouts, conv_core(): ahead_in[KERNEL - 1 - step_back:KERNEL - 1 - step_back + length]  37.2 us
    unnamed x490, local copies, waits for them, and re-layouts  37 us
    psum x1, blocking collectives, per_device(): grad_heads = lax.psum(grad_decay, ('seq', 'zero'))  31.7 us
    ppermute x4, starting transfers between devices, extended(): before = lax.ppermute(last, axis, up)  23.6 us
    add x12, other arithmetic, combine_states(): later[0][..., None, None] * earlier[1] + later[1]  22.9 us
    dot_general x12, matrix products, conv_core(): jnp.einsum('khij,kjhp->kihp', weights, values, preferred_element_type=jnp...  20.9 us
    dot_general x12, matrix products, conv_core(): jnp.einsum('khjn,kjhp->khnp', b_weighted, values, preferred_element_type=...  16.4 us
  transfers between devices with their start and end apart: 10, of which 0 were waited for; matrix products, arithmetic and copies ran while one was open for 18% of the time, Pallas kernels for 0%

profile of v1, /device:TPU:0, one launch (start us, length us, event | category | flops | bytes accessed | tf_op | source)
XLA Modules:
  0.0 753.5 jit_solution(7601086343714934292)
XLA Ops:
  7.2 8.7 %all-gather.14 = bf16[4,320,148]{1,2,0:T(8,128)(2,1)S(1)} all-gather(bf16[1,320,148]{1,2,0:T(8,128)(2,1)} %bitcast.1260), channel_id=1, replica_groups=mesh['grp'=2,'seq'=4,'zero'=4] {'zero'}, dimensions={0}, use_global_device_ids=true | all-gather | bytes 473600 | tf_op jit(solution)/shard_map/all_gather | solution.py:201
  62.7 9.2 %all-gather.6 = bf16[4,1,20,1]{2,3,1,0:T(2,128)(2,1)} all-gather(bf16[1,1,20,1]{2,3,1,0:T(2,128)(2,1)S(1)} %get-tuple-element.1334), channel_id=8, replica_groups=mesh['grp'=2,'seq'=4,'zero'=4] {'seq'}, dimensions={0}, use_global_device_ids=true | all-gather | bytes 200 | tf_op jit(solution)/shard_map/all_gather | solution.py:24
  71.8 8.1 %all-gather.4 = bf16[4,1,20,1]{2,3,1,0:T(2,128)(2,1)} all-gather(bf16[1,1,20,1]{2,3,1,0:T(2,128)(2,1)S(1)} %get-tuple-element.1331), channel_id=6, replica_groups=mesh['grp'=2,'seq'=4,'zero'=4] {'seq'}, dimensions={0}, use_global_device_ids=true | all-gather | bytes 200 | tf_op jit(solution)/shard_map/all_gather | solution.py:24
  80.0 9.2 %all-gather.2 = bf16[4,1,20,1]{2,3,1,0:T(2,128)(2,1)} all-gather(bf16[1,1,20,1]{2,3,1,0:T(2,128)(2,1)S(1)} %get-tuple-element.1328), channel_id=4, replica_groups=mesh['grp'=2,'seq'=4,'zero'=4] {'seq'}, dimensions={0}, use_global_device_ids=true | all-gather | bytes 200 | tf_op jit(solution)/shard_map/all_gather | solution.py:24
  89.2 8.6 %all-gather = bf16[4,1,20,1]{2,3,1,0:T(2,128)(2,1)} all-gather(bf16[1,1,20,1]{2,3,1,0:T(2,128)(2,1)S(1)} %get-tuple-element.1325), channel_id=2, replica_groups=mesh['grp'=2,'seq'=4,'zero'=4] {'seq'}, dimensions={0}, use_global_device_ids=true | all-gather | bytes 200 | tf_op jit(solution)/shard_map/all_gather | solution.py:24
  102.4 6.6 slice.395
  156.9 6.6 slice.366
  174.2 21.0 %all-gather.7 = bf16[80,64,64]{2,1,0:T(8,128)(2,1)} all-gather(bf16[20,64,64]{2,1,0:T(8,128)(2,1)S(1)} %fusion.28), channel_id=9, replica_groups=mesh['grp'=2,'seq'=4,'zero'=4] {'seq'}, dimensions={0}, use_global_device_ids=true | all-gather | bytes 819200 | tf_op jit(solution)/shard_map/all_gather | solution.py:24
  205.1 19.5 %all-gather.11 = bf16[4,20,64,64]{3,2,1,0:T(8,128)(2,1)} all-gather(bf16[1,20,64,64]{3,2,1,0:T(8,128)(2,1)} %copy.689), channel_id=13, replica_groups=mesh['grp'=2,'seq'=4,'zero'=4] {'seq'}, dimensions={0}, use_global_device_ids=true | all-gather | bytes 819200 | tf_op jit(solution)/shard_map/all_gather | solution.py:24
  240.9 23.6 %all-gather.3 = bf16[80,64,64]{2,1,0:T(8,128)(2,1)} all-gather(bf16[20,64,64]{2,1,0:T(8,128)(2,1)S(1)} %fusion.26), channel_id=5, replica_groups=mesh['grp'=2,'seq'=4,'zero'=4] {'seq'}, dimensions={0}, use_global_device_ids=true | all-gather | bytes 819200 | tf_op jit(solution)/shard_map/all_gather | solution.py:24
  265.5 8.5 %while.69 = (s32[]{:T(128)}, f32[1,20,64,64]{3,2,1,0:T(8,128)}, s32[]{:T(128)}, bf16[4,1,20]{2,1,0:T(2,128)(2,1)}, bf16[4,1,20,64,64]{4,3,2,1,0:T(8,128)(2,1)}, ...) while((s32[]{:T(128)}, f32[1,20,64,64]{3,2,1,0:T(8,128)}, s32[]{:T(128)}, bf16[4,1,20]{2,1,0:T(2,128)(2,1)}, ...), condition=%wide.region_5.7_spmd, body=%wide.region_4.6_spmd.sunk | while | flops 245786 | bytes 819555 | solution.py:41
  278.1 19.0 %all-gather.9 = bf16[4,20,64,64]{3,2,1,0:T(8,128)(2,1)} all-gather(bf16[1,20,64,64]{3,2,1,0:T(8,128)(2,1)} %copy.664), channel_id=11, replica_groups=mesh['grp'=2,'seq'=4,'zero'=4] {'seq'}, dimensions={0}, use_global_device_ids=true | all-gather | bytes 819200 | tf_op jit(solution)/shard_map/all_gather | solution.py:24
  341.7 29.2 %all-gather.10 = bf16[4,20,64,64]{3,2,1,0:T(8,128)(2,1)} all-gather(bf16[1,20,64,64]{3,2,1,0:T(8,128)(2,1)} %copy.684), channel_id=12, replica_groups=mesh['grp'=2,'seq'=4,'zero'=4] {'seq'}, dimensions={0}, use_global_device_ids=true | all-gather | bytes 819200 | tf_op jit(solution)/shard_map/all_gather | solution.py:24
  371.8 8.3 %while.74 = (s32[]{:T(128)}, f32[1,20,64,64]{3,2,1,0:T(8,128)}, s32[]{:T(128)}, bf16[4,1,20]{2,1,0:T(2,128)(2,1)}, bf16[4,1,20,64,64]{4,3,2,1,0:T(8,128)(2,1)}, ...) while((s32[]{:T(128)}, f32[1,20,64,64]{3,2,1,0:T(8,128)}, s32[]{:T(128)}, bf16[4,1,20]{2,1,0:T(2,128)(2,1)}, ...), condition=%wide.region_44.46_spmd, body=%wide.region_43.45_spmd.sunk | while | flops 245786 | bytes 819555 | solution.py:41
  394.9 20.7 %all-gather.8 = bf16[4,20,64,64]{3,2,1,0:T(8,128)(2,1)} all-gather(bf16[1,20,64,64]{3,2,1,0:T(8,128)(2,1)} %copy.659), channel_id=10, replica_groups=mesh['grp'=2,'seq'=4,'zero'=4] {'seq'}, dimensions={0}, use_global_device_ids=true | all-gather | bytes 819200 | tf_op jit(solution)/shard_map/all_gather | solution.py:24
  416.5 8.2 %while.72 = (s32[]{:T(128)}, f32[1,20,64,64]{3,2,1,0:T(8,128)}, s32[]{:T(128)}, bf16[4,1,20]{2,1,0:T(2,128)(2,1)}, bf16[4,1,20,64,64]{4,3,2,1,0:T(8,128)(2,1)}, ...) while((s32[]{:T(128)}, f32[1,20,64,64]{3,2,1,0:T(8,128)}, s32[]{:T(128)}, bf16[4,1,20]{2,1,0:T(2,128)(2,1)}, ...), condition=%wide.region_14.16_spmd, body=%wide.region_13.15_spmd.sunk | while | flops 245786 | bytes 819555 | solution.py:41
  429.2 21.7 %all-gather.5 = bf16[80,64,64]{2,1,0:T(8,128)(2,1)} all-gather(bf16[20,64,64]{2,1,0:T(8,128)(2,1)S(1)} %fusion.27), channel_id=7, replica_groups=mesh['grp'=2,'seq'=4,'zero'=4] {'seq'}, dimensions={0}, use_global_device_ids=true | all-gather | bytes 819200 | tf_op jit(solution)/shard_map/all_gather | solution.py:24
  453.2 27.1 %all-gather.1 = bf16[80,64,64]{2,1,0:T(8,128)(2,1)} all-gather(bf16[20,64,64]{2,1,0:T(8,128)(2,1)S(1)} %fusion.25), channel_id=3, replica_groups=mesh['grp'=2,'seq'=4,'zero'=4] {'seq'}, dimensions={0}, use_global_device_ids=true | all-gather | bytes 819200 | tf_op jit(solution)/shard_map/all_gather | solution.py:24
  505.5 8.0 %reverse.8 = f32[1,256,1408]{1,2,0:T(8,128)} reverse(f32[1,256,1408]{1,2,0:T(8,128)S(1)} %bitcast.1188), dimensions={1} | reverse | bytes 2883584
  524.0 12.5 %reverse.9 = f32[1,256,1408]{1,2,0:T(8,128)} reverse(f32[1,256,1408]{1,2,0:T(8,128)} %bitcast.1189), dimensions={1} | reverse | bytes 2883584
  590.5 6.9 collective-permute-start.6
  685.3 31.7 %psum.15 = f32[2,20]{1,0:T(2,128)} all-reduce(f32[2,20]{1,0:T(2,128)S(1)} %maximum_add_fusion), channel_id=1, replica_groups=mesh['grp'=2,'seq'=4,'zero'=4] {'seq','zero'}, use_global_device_ids=true, to_apply=%region_100.102 | all-reduce | flops 40 | bytes 320 | tf_op jit(solution)/shard_map/psum | solution.py:231
  720.0 8.4 %psum.14 = bf16[4,352]{1,0:T(4,128)(2,1)S(1)} all-reduce(bf16[4,352]{1,0:T(4,128)(2,1)S(1)} %copy.719), channel_id=1, replica_groups=mesh['grp'=2,'seq'=4,'zero'=4] {'seq'}, use_global_device_ids=true, to_apply=%region_91.93 | all-reduce | flops 1408 | bytes 5632 | tf_op jit(solution)/shard_map/psum | solution.py:229
  730.1 15.6 %all-gather.15 = bf16[4,320,148]{1,2,0:T(8,128)(2,1)S(1)} all-gather(bf16[1,320,148]{1,2,0:T(8,128)(2,1)S(1)} %bitcast.1257), channel_id=14, replica_groups=mesh['grp'=2,'seq'=4,'zero'=4] {'seq'}, dimensions={0}, use_global_device_ids=true | all-gather | bytes 473600 | tf_op jit(solution)/shard_map/all_gather | solution.py:15
  (817 shorter events, 419.9 us)
Async XLA Ops:
  7.2 711.9 %reduce-scatter.9.cloned.1.call-start = ((), (), s32[]{:S(2)}) async-start(), calls=%async_computation.3 | async-start | bytes 450560
  18.1 106.1 %collective-permute-start.1 = (bf16[1,3,1408]{1,2,0:T(8,128)(2,1)}, bf16[1,3,1408]{1,2,0:T(8,128)(2,1)}, u32[]{:S(2)}, u32[]{:S(2)}) collective-permute-start(bf16[1,3,1408]{1,2,0:T(8,128)(2,1)} %get-tuple-element.1305), channel_id=1, source_target_pairs={{4,0},{8,4},{12,8},{5,1},{9,5},{13,9},{6,2},{10,6},{14,10},{7,3},{... | collective-permute-start | bytes 25352 | tf_op jit(solution)/shard_map/ppermute | solution.py:52
  19.4 104.8 %collective-permute-start = (bf16[1,3,1408]{1,2,0:T(8,128)(2,1)}, bf16[1,3,1408]{1,2,0:T(8,128)(2,1)}, u32[]{:S(2)}, u32[]{:S(2)}) collective-permute-start(bf16[1,3,1408]{1,2,0:T(8,128)(2,1)} %get-tuple-element.1304), channel_id=1, source_target_pairs={{0,4},{4,8},{8,12},{1,5},{5,9},{9,13},{2,6},{6,10},{10,14},{3,7},{... | collective-permute-start | bytes 25352 | tf_op jit(solution)/shard_map/ppermute | solution.py:51
  25.1 72.8 %copy-start.25 = (bf16[1,128,1280]{1,2,0:T(8,128)(2,1)}, bf16[1,128,1280]{1,2,0:T(8,128)(2,1)S(1)}, u32[]{:S(2)}) copy-start(bf16[1,128,1280]{1,2,0:T(8,128)(2,1)S(1)} %rev.50) | copy-start | bytes 983044
  26.6 71.3 %collective-permute-start.3 = (bf16[1,3,1408]{1,2,0:T(8,128)(2,1)}, bf16[1,3,1408]{1,2,0:T(8,128)(2,1)}, u32[]{:S(2)}, u32[]{:S(2)}) collective-permute-start(bf16[1,3,1408]{1,2,0:T(8,128)(2,1)} %get-tuple-element.1307), channel_id=1, source_target_pairs={{4,0},{8,4},{12,8},{5,1},{9,5},{13,9},{6,2},{10,6},{14,10},{7,3},{... | collective-permute-start | bytes 25352 | tf_op jit(solution)/shard_map/ppermute | solution.py:52
  27.8 70.0 %collective-permute-start.2 = (bf16[1,3,1408]{1,2,0:T(8,128)(2,1)}, bf16[1,3,1408]{1,2,0:T(8,128)(2,1)}, u32[]{:S(2)}, u32[]{:S(2)}) collective-permute-start(bf16[1,3,1408]{1,2,0:T(8,128)(2,1)} %get-tuple-element.1306), channel_id=1, source_target_pairs={{0,4},{4,8},{8,12},{1,5},{5,9},{9,13},{2,6},{6,10},{10,14},{3,7},{... | collective-permute-start | bytes 25352 | tf_op jit(solution)/shard_map/ppermute | solution.py:51
  33.6 23.7 %copy-start.52 = (f32[1,1,128,20]{3,2,1,0:T(8,128)}, f32[1,1,128,20]{3,2,1,0:T(8,128)S(1)}, u32[]{:S(2)}) copy-start(f32[1,1,128,20]{3,2,1,0:T(8,128)S(1)} %reduce_window_sum.90) | copy-start | bytes 30724
  35.9 24.7 %copy-start.54 = (f32[1,1,128,20]{3,2,1,0:T(8,128)}, f32[1,1,128,20]{3,2,1,0:T(8,128)S(1)}, u32[]{:S(2)}) copy-start(f32[1,1,128,20]{3,2,1,0:T(8,128)S(1)} %reduce_window_sum.86) | copy-start | bytes 30724
  38.7 22.6 %copy-start.58 = (f32[1,1,128,20]{3,2,1,0:T(8,128)}, f32[1,1,128,20]{3,2,1,0:T(8,128)S(1)}, u32[]{:S(2)}) copy-start(f32[1,1,128,20]{3,2,1,0:T(8,128)S(1)} %reduce_window_sum.84) | copy-start | bytes 30724
  45.3 80.6 %copy-start.134 = (f32[1408]{0:T(1024)}, f32[1408]{0:T(1024)S(1)}, u32[]{:S(2)}) copy-start(f32[1408]{0:T(1024)S(1)} %get-tuple-element.1150) | copy-start | bytes 16900
  45.3 80.6 %copy-start.136 = (f32[1408]{0:T(1024)}, f32[1408]{0:T(1024)S(1)}, u32[]{:S(2)}) copy-start(f32[1408]{0:T(1024)S(1)} %get-tuple-element.1151) | copy-start | bytes 16900
  200.8 23.8 %copy-start.2 = (f32[1,20,64,64]{3,2,1,0:T(8,128)}, f32[1,20,64,64]{3,2,1,0:T(8,128)S(1)}, u32[]{:S(2)}) copy-start(f32[1,20,64,64]{3,2,1,0:T(8,128)S(1)} %get-tuple-element.760) | copy-start | bytes 983044
  587.9 27.3 %copy-start.59 = (f32[1,1,128,20]{3,2,1,0:T(8,128)S(1)}, f32[1,1,128,20]{3,2,1,0:T(8,128)}, u32[]{:S(2)}) copy-start(f32[1,1,128,20]{3,2,1,0:T(8,128)} %copy-done.58) | copy-start | bytes 30724
  588.0 27.3 %copy-start.109 = (f32[1,128,148]{2,1,0:T(8,128)S(1)}, f32[1,128,148]{2,1,0:T(8,128)}, u32[]{:S(2)}) copy-start(f32[1,128,148]{2,1,0:T(8,128)} %copy-done.108) | copy-start | bytes 227332
  588.0 27.3 %copy-start.195 = (f32[20]{0:T(128)S(1)}, f32[20]{0:T(128)}, u32[]{:S(2)}) copy-start(f32[20]{0:T(128)} %get-tuple-element.1326) | copy-start | bytes 244
  589.0 25.0 %copy-start.133 = (f32[1,1,128,20]{3,2,1,0:T(8,128)S(1)}, f32[1,1,128,20]{3,2,1,0:T(8,128)}, u32[]{:S(2)}) copy-start(f32[1,1,128,20]{3,2,1,0:T(8,128)} %get-tuple-element.1367) | copy-start | bytes 30724
  589.0 27.6 %copy-start.57 = (f32[1,1,128,20]{3,2,1,0:T(8,128)S(1)}, f32[1,1,128,20]{3,2,1,0:T(8,128)}, u32[]{:S(2)}) copy-start(f32[1,1,128,20]{3,2,1,0:T(8,128)} %copy-done.56) | copy-start | bytes 30724
  589.0 27.6 %copy-start.103 = (f32[1,128,148]{2,1,0:T(8,128)S(1)}, f32[1,128,148]{2,1,0:T(8,128)}, u32[]{:S(2)}) copy-start(f32[1,128,148]{2,1,0:T(8,128)} %copy-done.102) | copy-start | bytes 227332
  589.1 61.9 %collective-permute-start.7 = (bf16[1,3,1408]{1,2,0:T(8,128)(2,1)}, bf16[1,3,1408]{1,2,0:T(8,128)(2,1)}, u32[]{:S(2)}, u32[]{:S(2)}) collective-permute-start(bf16[1,3,1408]{1,2,0:T(8,128)(2,1)} %get-tuple-element.1271), channel_id=1, source_target_pairs={{4,0},{8,4},{12,8},{5,1},{9,5},{13,9},{6,2},{10,6},{14,10},{7,3},{... | collective-permute-start | bytes 25352 | tf_op jit(solution)/shard_map/ppermute | solution.py:52
  590.5 60.5 %collective-permute-start.6 = (bf16[1,3,1408]{1,2,0:T(8,128)(2,1)}, bf16[1,3,1408]{1,2,0:T(8,128)(2,1)}, u32[]{:S(2)}, u32[]{:S(2)}) collective-permute-start(bf16[1,3,1408]{1,2,0:T(8,128)(2,1)} %get-tuple-element.1270), channel_id=1, source_target_pairs={{0,4},{4,8},{8,12},{1,5},{5,9},{9,13},{2,6},{6,10},{10,14},{3,7},{... | collective-permute-start | bytes 25352 | tf_op jit(solution)/shard_map/ppermute | solution.py:51
  605.2 62.0 %collective-permute-start.5 = (bf16[1,3,1408]{1,2,0:T(8,128)(2,1)}, bf16[1,3,1408]{1,2,0:T(8,128)(2,1)}, u32[]{:S(2)}, u32[]{:S(2)}) collective-permute-start(bf16[1,3,1408]{1,2,0:T(8,128)(2,1)} %get-tuple-element.1269), channel_id=1, source_target_pairs={{4,0},{8,4},{12,8},{5,1},{9,5},{13,9},{6,2},{10,6},{14,10},{7,3},{... | collective-permute-start | bytes 25352 | tf_op jit(solution)/shard_map/ppermute | solution.py:52
  606.5 60.7 %collective-permute-start.4 = (bf16[1,3,1408]{1,2,0:T(8,128)(2,1)}, bf16[1,3,1408]{1,2,0:T(8,128)(2,1)}, u32[]{:S(2)}, u32[]{:S(2)}) collective-permute-start(bf16[1,3,1408]{1,2,0:T(8,128)(2,1)} %get-tuple-element.1268), channel_id=1, source_target_pairs={{0,4},{4,8},{8,12},{1,5},{5,9},{9,13},{2,6},{6,10},{10,14},{3,7},{... | collective-permute-start | bytes 25352 | tf_op jit(solution)/shard_map/ppermute | solution.py:51
  638.5 90.5 %reduce-scatter.7.cloned.1.call-start = ((), (), s32[]{:S(2)}) async-start(), calls=%async_computation.2 | async-start | bytes 819200
  683.7 33.4 %copy-start.24 = (bf16[1280,148]{0,1:T(8,128)(2,1)S(1)}, bf16[1280,148]{0,1:T(8,128)(2,1)}, u32[]{:S(2)}) copy-start(bf16[1280,148]{0,1:T(8,128)(2,1)} %copy-done.23) | copy-start | bytes 1136644
  (225 other events, 1192.5 us)
Sparse Core Ops, SparseCore 0:
  638.6 24.8 reduce-scatter.8
  685.3 26.7 reduce-scatter.6
